TPU v7x, 128 devices: a whole 4x4x4 slice. The times are simulated.
128 devices in a mesh: pair: 2 (over core), batch: 4 (over y), vocab: 16 (over x, z).
Axes of the slice: x: 4, y: 4, z: 4, core: 2. Of those that a mesh axis runs over, the one named last changes fastest.
Arguments:
- hidden: bfloat16 [2, 512, 8192], P('pair', 'batch', 'vocab'), may hold values from -120 to 120
- norm_gain: bfloat16 [8192], P('vocab'), may hold values from 0.099609375 to 1.8984375
- head_weight: bfloat16 [8192, 65536], P(('pair', 'batch'), 'vocab'), may hold values from -1 to 1
Outputs:
- guided_logprobs: float32 [512, 65536], P(('pair', 'batch'), 'vocab')
- cond_logprobs: float32 [512, 65536], P(('pair', 'batch'), 'vocab')
All inputs are finite; a program needn't handle non-finite values.
Results may differ from a plain program's by a relative error of at most 0.007.
Values may be sent and summed in bfloat16 or wider, within the bound.
A program may use at most 128 MiB of HBM per device.

v0:
```python
import jax
import jax.numpy as jnp
from jax import lax
from jax.sharding import PartitionSpec as P

D = 8192
EPS = 1e-05
GUIDE = 1.5


def on_device(hidden, norm_gain, head_weight):
    rows = hidden[0]
    wide = rows.astype(jnp.float32)
    partial_sq = jnp.sum(wide * wide, axis=1)
    total_sq = lax.psum(partial_sq, "vocab")
    scaled = wide * lax.rsqrt(total_sq / D + EPS)[:, None] * norm_gain.astype(jnp.float32)[None, :]
    features = lax.all_gather(scaled.astype(jnp.bfloat16), "vocab", axis=1, tiled=True)
    blocks = lax.all_to_all(features, ("pair", "batch"), split_axis=1, concat_axis=0, tiled=True)
    groups = lax.axis_size("pair") * lax.axis_size("batch")
    width = blocks.shape[1]
    out_rows = blocks.shape[0] // (2 * groups)
    ordered = blocks.reshape(2, groups, out_rows, width).transpose(1, 0, 2, 3).reshape(-1, width)
    logits = lax.psum_scatter(
        jnp.dot(ordered, head_weight, preferred_element_type=jnp.float32),
        ("pair", "batch"),
        scatter_dimension=0,
        tiled=True,
    )
    cond = logits[:out_rows]
    uncond = logits[out_rows:]
    guided = GUIDE * cond + (1.0 - GUIDE) * uncond
    peak_c, peak_g = lax.pmax((jnp.max(cond, axis=1), jnp.max(guided, axis=1)), "vocab")
    local_c = jnp.sum(jnp.exp(cond - peak_c[:, None]), axis=1)
    local_g = jnp.sum(jnp.exp(guided - peak_g[:, None]), axis=1)
    total_c, total_g = lax.psum((local_c, local_g), "vocab")
    cond_out = cond - (peak_c + jnp.log(total_c))[:, None]
    guided_out = guided - (peak_g + jnp.log(total_g))[:, None]
    return (guided_out, cond_out)


def solution(mesh):
    in_specs = (P("pair", "batch", "vocab"), P("vocab"), P(("pair", "batch"), "vocab"))
    out_specs = (P(("pair", "batch"), "vocab"), P(("pair", "batch"), "vocab"))
    return jax.shard_map(
        on_device, mesh=mesh, in_specs=in_specs, out_specs=out_specs, check_vma=False
    )
```

profile of v0, /device:TPU:32, one launch (start us, length us, event | category | flops | bytes accessed | tf_op | source)
XLA Modules:
  0.0 398.5 jit_solution(13088770015210042575)
XLA Ops:
  7.2 0.0 all-gather.2.cloned.1.call-start
  7.2 0.7 convert_element_type.14
  7.9 1.0 copy.6
  8.9 0.1 fusion.1
  9.0 36.8 %psum.21 = f32[128]{0:T(128)S(1)} all-reduce(f32[128]{0:T(128)S(1)} %fusion.1), channel_id=1, replica_groups=mesh['pair'=2,'batch'=4,'vocab'=16] {'vocab'}, use_global_device_ids=true, to_apply=%region_1.0 | all-reduce | flops 128 | bytes 1024 | tf_op jit(solution)/shard_map/psum | solution.py:15
  45.9 0.8 fusion.3
  46.7 0.0 all-gather.2.cloned.1.call-update
  46.7 0.0 reduce-scatter.2.cloned.1.call-start
  46.7 45.9 %all-gather.2.cloned.1.call-done = bf16[128,8192]{0,1:T(8,128)(2,1)} async-done(((bf16[128,512]{0,1:T(8,128)(2,1)}), bf16[128,8192]{0,1:T(8,128)(2,1)}) %all-gather.2.cloned.1.call-update) | async-done | bytes 2097168 | tf_op jit(solution)/shard_map/all_gather | solution.py:17
  92.7 30.9 %all_to_all.16 = bf16[128,8,1024]{0,2,1:T(8,128)(2,1)S(1)} all-to-all(bf16[128,8,1024]{0,2,1:T(8,128)(2,1)} %bitcast.14), channel_id=1, replica_groups=mesh['pair'=2,'batch'=4,'vocab'=16] {'pair','batch'}, dimensions={1} | all-to-all | bytes 4194304 | tf_op jit(solution)/shard_map/all_to_all | solution.py:18
  123.5 2.6 copy.7
  126.1 1.8 copy.8
  127.9 14.4 %fusion.5 = f32[1024,4096]{1,0:T(8,128)} fusion(bf16[1024,1024]{1,0:T(8,128)(2,1)S(1)} %bitcast.15, bf16[1024,4096]{1,0:T(8,128)(2,1)} %param.5), kind=kOutput, calls=%fused_computation.16 | convolution fusion | flops 8589934592 | bytes 27262976 | tf_op jit(solution)/shard_map/dot_general | solution.py:24
  142.4 0.0 reduce-scatter.2.cloned.1.call-update
  142.4 168.8 %reduce-scatter.2.cloned.1.call-done = f32[128,4096]{1,0:T(8,128)} async-done(((f32[1024,4096]{1,0:T(8,128)}), f32[128,4096]{1,0:T(8,128)}) %reduce-scatter.2.cloned.1.call-update) | async-done | bytes 2097168 | tf_op jit(solution)/shard_map/reduce_scatter | solution.py:23
  311.1 0.0 copy-start
  311.1 2.0 slice_reduce_fusion
  313.1 36.4 %all-reduce.1 = (f32[64]{0:T(128)S(1)}, f32[64]{0:T(128)S(1)}) all-reduce(f32[64]{0:T(128)S(1)} %get-tuple-element.5, f32[64]{0:T(128)S(1)} %get-tuple-element.4), channel_id=1, replica_groups=mesh['pair'=2,'batch'=4,'vocab'=16] {'vocab'}, use_global_device_ids=true, to_apply=%region_4.0 | all-reduce | flops 128 | bytes 1024 | tf_op jit(solution)/shard_map/pmax | solution.py:32
  349.5 0.0 copy-done
  349.5 0.5 exponential_reduce_fusion
  350.1 40.0 %all-reduce = (f32[64]{0:T(128)S(1)}, f32[64]{0:T(128)S(1)}) all-reduce(f32[64]{0:T(128)S(1)} %get-tuple-element.3, f32[64]{0:T(128)S(1)} %get-tuple-element.2), channel_id=1, replica_groups=mesh['pair'=2,'batch'=4,'vocab'=16] {'vocab'}, use_global_device_ids=true, to_apply=%region_6.0 | all-reduce | flops 128 | bytes 1024 | tf_op jit(solution)/shard_map/psum | solution.py:35
  390.1 1.6 slice_subtract_fusion
  (2 shorter events, 0.0 us)
Async XLA Ops:
  7.2 85.5 %all-gather.2.cloned.1.call-start = ((), (), s32[]{:S(2)}) async-start(), calls=%async_computation.2 | async-start | bytes 2228224 | tf_op jit(solution)/shard_map/all_gather | solution.py:17
  46.7 264.5 %reduce-scatter.2.cloned.1.call-start = ((), (), s32[]{:S(2)}) async-start(), calls=%async_computation.3 | async-start | bytes 18874368 | tf_op jit(solution)/shard_map/reduce_scatter | solution.py:23
  311.1 38.4 %copy-start = (f32[128,4096]{1,0:T(8,128)S(1)}, f32[128,4096]{1,0:T(8,128)}, u32[]{:S(2)}) copy-start(f32[128,4096]{1,0:T(8,128)} %reduce-scatter.2.cloned.1.call-done) | copy-start | bytes 6291460
Sparse Core Ops, SparseCore 0:
  46.8 45.8 all-gather.1
  142.5 168.5 reduce-scatter.1
where the time goes:
time: 399 us
  waiting for transfers between devices  215 us (54%)
  blocking collectives  144 us (36%)
  matrix products  14.4 us (4%)
  between operations  14.1 us (4%)
  other arithmetic  5.68 us (1%)
  local copies, waits for them, and re-layouts  5.44 us (1%)
    reduce_scatter x1, waiting for transfers between devices, on_device(): lax.psum_scatter(jnp.dot(ordered, head_weight, preferred_element_type=jnp...  169 us
    all_gather x1, waiting for transfers between devices, on_device(): lax.all_gather(scaled.astype(jnp.bfloat16), 'vocab', axis=1, tiled=True)  45.9 us
    psum x1, blocking collectives, on_device(): total_c, total_g = lax.psum((local_c, local_g), 'vocab')  40 us
    psum x1, blocking collectives, on_device(): total_sq = lax.psum(partial_sq, 'vocab')  36.8 us
    pmax x1, blocking collectives, on_device(): lax.pmax((jnp.max(cond, axis=1), jnp.max(guided, axis=1)), 'vocab')  36.4 us
    all_to_all x1, blocking collectives, on_device(): lax.all_to_all(features, ('pair', 'batch'), split_axis=1, concat_axis=0,...  30.9 us
    dot_general x1, matrix products, on_device(): jnp.dot(ordered, head_weight, preferred_element_type=jnp.float32)  14.4 us
  transfers between devices with their start and end apart: 2, of which 2 were waited for; matrix products, arithmetic and copies ran while one was open for 0% of the time, Pallas kernels for 0%

commit v1 on v0

--- a/solution.py
+++ b/solution.py
@@ -2,6 +2,7 @@
 import jax.numpy as jnp
 from jax import lax
 from jax.sharding import PartitionSpec as P
+from jax.lax import all_gather
 
 D = 8192
 EPS = 1e-05
@@ -12,7 +13,12 @@
     rows = hidden[0]
     wide = rows.astype(jnp.float32)
     partial_sq = jnp.sum(wide * wide, axis=1)
-    total_sq = lax.psum(partial_sq, "vocab")
+
+    def _fill_cards(x_part):
+        r_now = jnp.sum(all_gather(x_part, "vocab"), axis=0)
+        return r_now
+
+    total_sq = _fill_cards(partial_sq)
     scaled = wide * lax.rsqrt(total_sq / D + EPS)[:, None] * norm_gain.astype(jnp.float32)[None, :]
     features = lax.all_gather(scaled.astype(jnp.bfloat16), "vocab", axis=1, tiled=True)
     blocks = lax.all_to_all(features, ("pair", "batch"), split_axis=1, concat_axis=0, tiled=True)

time: 399 us -> 382 us (0.957)
  blocking collectives: 144 us -> 129 us
    psum x1 -> x0, blocking collectives: 36.8 us -> none  [on_device(): total_sq = lax.psum(partial_sq, 'vocab')]
    all_gather x0 -> x1, blocking collectives: none -> 21.2 us  [_fill_cards(): r_now = jnp.sum(all_gather(x_part, 'vocab'), axis=0)]
where the time goes in v1:
time: 382 us
  waiting for transfers between devices  214 us (56%)
  blocking collectives  129 us (34%)
  matrix products  14.4 us (4%)
  between operations  14.1 us (4%)
  other arithmetic  5.71 us (1%)
  local copies, waits for them, and re-layouts  5.44 us (1%)
    reduce_scatter x1, waiting for transfers between devices, on_device(): lax.psum_scatter(jnp.dot(ordered, head_weight, preferred_element_type=jnp...  169 us
    all_gather x1, waiting for transfers between devices, on_device(): lax.all_gather(scaled.astype(jnp.bfloat16), 'vocab', axis=1, tiled=True)  45.1 us
    psum x1, blocking collectives, on_device(): total_c, total_g = lax.psum((local_c, local_g), 'vocab')  40 us
    pmax x1, blocking collectives, on_device(): lax.pmax((jnp.max(cond, axis=1), jnp.max(guided, axis=1)), 'vocab')  36.4 us
    all_to_all x1, blocking collectives, on_device(): lax.all_to_all(features, ('pair', 'batch'), split_axis=1, concat_axis=0,...  30.9 us
    all_gather x1, blocking collectives, _fill_cards(): r_now = jnp.sum(all_gather(x_part, 'vocab'), axis=0)  21.2 us
    dot_general x1, matrix products, on_device(): jnp.dot(ordered, head_weight, preferred_element_type=jnp.float32)  14.4 us
  transfers between devices with their start and end apart: 2, of which 2 were waited for; matrix products, arithmetic and copies ran while one was open for 0% of the time, Pallas kernels for 0%

profile of v1, /device:TPU:32, one launch (start us, length us, event | category | flops | bytes accessed | tf_op | source)
XLA Modules:
  0.0 382.1 jit_solution(992642435925621733)
XLA Ops:
  7.2 0.0 all-gather.4.cloned.1.call-start
  7.2 0.7 convert_element_type.14
  7.9 1.0 copy.9
  8.9 0.1 fusion.1
  9.0 21.2 %all-gather.1 = f32[16,1,128]{2,1,0:T(1,128)S(1)} all-gather(f32[1,1,128]{2,1,0:T(1,128)S(1)} %bitcast.17), channel_id=2, replica_groups=mesh['pair'=2,'batch'=4,'vocab'=16] {'vocab'}, dimensions={0}, use_global_device_ids=true | all-gather | bytes 8704 | tf_op jit(solution)/shard_map/all_gather | solution.py:18
  30.3 0.8 fusion.3
  31.1 0.0 all-gather.4.cloned.1.call-update
  31.1 0.0 reduce-scatter.2.cloned.1.call-start
  31.1 45.1 %all-gather.4.cloned.1.call-done = bf16[128,8192]{0,1:T(8,128)(2,1)} async-done(((bf16[128,512]{0,1:T(8,128)(2,1)}), bf16[128,8192]{0,1:T(8,128)(2,1)}) %all-gather.4.cloned.1.call-update) | async-done | bytes 2097168 | tf_op jit(solution)/shard_map/all_gather | solution.py:23
  76.2 30.9 %all_to_all.16 = bf16[128,8,1024]{0,2,1:T(8,128)(2,1)S(1)} all-to-all(bf16[128,8,1024]{0,2,1:T(8,128)(2,1)} %bitcast.15), channel_id=1, replica_groups=mesh['pair'=2,'batch'=4,'vocab'=16] {'pair','batch'}, dimensions={1} | all-to-all | bytes 4194304 | tf_op jit(solution)/shard_map/all_to_all | solution.py:24
  107.1 2.6 copy.10
  109.7 1.8 copy.11
  111.5 14.4 %fusion.5 = f32[1024,4096]{1,0:T(8,128)} fusion(bf16[1024,1024]{1,0:T(8,128)(2,1)S(1)} %bitcast.16, bf16[1024,4096]{1,0:T(8,128)(2,1)} %param.5), kind=kOutput, calls=%fused_computation.16 | convolution fusion | flops 8589934592 | bytes 27262976 | tf_op jit(solution)/shard_map/dot_general | solution.py:30
  125.9 0.0 reduce-scatter.2.cloned.1.call-update
  125.9 168.8 %reduce-scatter.2.cloned.1.call-done = f32[128,4096]{1,0:T(8,128)} async-done(((f32[1024,4096]{1,0:T(8,128)}), f32[128,4096]{1,0:T(8,128)}) %reduce-scatter.2.cloned.1.call-update) | async-done | bytes 2097168 | tf_op jit(solution)/shard_map/reduce_scatter | solution.py:29
  294.7 0.0 copy-start
  294.7 2.0 slice_reduce_fusion
  296.6 36.4 %all-reduce.1 = (f32[64]{0:T(128)S(1)}, f32[64]{0:T(128)S(1)}) all-reduce(f32[64]{0:T(128)S(1)} %get-tuple-element.5, f32[64]{0:T(128)S(1)} %get-tuple-element.4), channel_id=1, replica_groups=mesh['pair'=2,'batch'=4,'vocab'=16] {'vocab'}, use_global_device_ids=true, to_apply=%region_4.0 | all-reduce | flops 128 | bytes 1024 | tf_op jit(solution)/shard_map/pmax | solution.py:38
  333.1 0.0 copy-done
  333.1 0.5 exponential_reduce_fusion
  333.6 40.0 %all-reduce = (f32[64]{0:T(128)S(1)}, f32[64]{0:T(128)S(1)}) all-reduce(f32[64]{0:T(128)S(1)} %get-tuple-element.3, f32[64]{0:T(128)S(1)} %get-tuple-element.2), channel_id=1, replica_groups=mesh['pair'=2,'batch'=4,'vocab'=16] {'vocab'}, use_global_device_ids=true, to_apply=%region_6.0 | all-reduce | flops 128 | bytes 1024 | tf_op jit(solution)/shard_map/psum | solution.py:41
  373.6 1.6 slice_subtract_fusion
  (3 shorter events, 0.1 us)
Async XLA Ops:
  7.2 69.0 %all-gather.4.cloned.1.call-start = ((), (), s32[]{:S(2)}) async-start(), calls=%async_computation.2 | async-start | bytes 2228224 | tf_op jit(solution)/shard_map/all_gather | solution.py:23
  31.1 263.6 %reduce-scatter.2.cloned.1.call-start = ((), (), s32[]{:S(2)}) async-start(), calls=%async_computation.3 | async-start | bytes 18874368 | tf_op jit(solution)/shard_map/reduce_scatter | solution.py:29
  294.7 38.4 %copy-start = (f32[128,4096]{1,0:T(8,128)S(1)}, f32[128,4096]{1,0:T(8,128)}, u32[]{:S(2)}) copy-start(f32[128,4096]{1,0:T(8,128)} %reduce-scatter.2.cloned.1.call-done) | copy-start | bytes 6291460
Sparse Core Ops, SparseCore 0:
  31.2 44.9 all-gather.3
  126.0 168.5 reduce-scatter.1
